TPU v7x, 256 devices: a whole 4x4x8 slice. The times are simulated.
256 devices in a mesh: expert: 8 (over x, core), dp: 8 (over z), pipe: 4 (over y).
Axes of the slice: x: 4, y: 4, z: 8, core: 2. Of those that a mesh axis runs over, the one named last changes fastest.
Arguments:
- tokens: bfloat16 [2048, 3072], P(('expert', 'dp'), 'pipe'), may hold values from -6 to 6
- out_grad: bfloat16 [2048, 3072], P(('expert', 'dp'), 'pipe'), may hold values from -6 to 6
- gate_values: float32 [2048, 2], P(('expert', 'dp')), may hold values from 0.1 to 1
- expert_ids: int32 [2048, 2], P(('expert', 'dp')), may hold values from 0 to 7, all different within a row; in each aligned block of 32 rows (0 to 31, 32 to 63, ...) at most 16 rows name the same one
- w_gate: bfloat16 [8, 3072, 8192], P('expert', None, ('dp', 'pipe')), may hold values from -0.109375 to 0.109375
- w_up: bfloat16 [8, 3072, 8192], P('expert', None, ('dp', 'pipe')), may hold values from -0.109375 to 0.109375
- w_down: bfloat16 [8, 8192, 3072], P('expert', ('dp', 'pipe')), may hold values from -0.0625 to 0.0625
Outputs:
- grad_tokens: bfloat16 [2048, 3072], P(('expert', 'dp'), 'pipe')
- gate_weight_gradient: bfloat16 [8, 3072, 8192], P('expert', None, ('dp', 'pipe'))
- up_weight_gradient: bfloat16 [8, 3072, 8192], P('expert', None, ('dp', 'pipe'))
- grad_down: bfloat16 [8, 8192, 3072], P('expert', ('dp', 'pipe'))
Inputs may be any that keep to these rules, and one draw needn't show every extreme that they name: `expert_ids`: each token names two different experts; among the 32 tokens of one block no expert is named more than 16 times, and in some blocks one is named exactly 16 times.
All inputs are finite; a program needn't handle non-finite values.
Results may differ from a plain program's by a relative error of at most 0.0065.
Values may be sent and summed in bfloat16 or wider, within the bound.
No kernel may reach another device: no remote copies, remote signals or barrier semaphores. Data moves between devices by JAX's collectives and lax.ppermute only.
A program may use at most 128 MiB of HBM per device.

v0:
```python
import jax
import jax.numpy as jnp
from jax import lax
from jax.sharding import PartitionSpec as P


def dispatch_tables(expert_ids, gate_values, expert_count, capacity):
    token_count = expert_ids.shape[0]
    choices_flat = expert_ids.reshape(-1)
    one_hot = (choices_flat[:, None] == jnp.arange(expert_count, dtype=jnp.int32)[None, :]).astype(
        jnp.int32
    )
    ranks = jnp.cumsum(one_hot, axis=0) - 1
    slot_index = choices_flat * capacity + jnp.sum(one_hot * ranks, axis=1)
    hits = jnp.arange(expert_count * capacity, dtype=jnp.int32)[:, None] == slot_index[None, :]
    hits = hits.reshape(expert_count * capacity, token_count, 2)
    picker = jnp.any(hits, axis=2).astype(jnp.bfloat16)
    weighting = jnp.sum(jnp.where(hits, gate_values[None, :, :], 0.0), axis=2)
    return (picker, weighting)


def fill_slots(picker, weighting, features, cotangent):
    sent_rows = jnp.dot(picker, features, preferred_element_type=jnp.float32).astype(jnp.bfloat16)
    sent_grads = jnp.dot(
        weighting, cotangent.astype(jnp.float32), precision=lax.Precision.HIGHEST
    ).astype(jnp.bfloat16)
    return (sent_rows, sent_grads)


def body(tokens, out_grad, gate_values, expert_ids, w_gate, w_up, w_down):
    expert_count = lax.axis_size("expert")
    group_count = lax.axis_size("dp")
    pipe_count = lax.axis_size("pipe")
    token_count = tokens.shape[0]
    capacity = max(token_count // 2, 2 * token_count // expert_count)
    slot_total = expert_count * capacity
    feat_part = tokens.shape[1]
    model_width = feat_part * pipe_count
    hidden_part = w_gate.shape[2]
    picker, weighting = dispatch_tables(expert_ids, gate_values, expert_count, capacity)
    sent_rows, sent_grads = fill_slots(picker, weighting, tokens, out_grad)
    recv_rows, recv_grads = (
        lax.all_to_all(
            sent_rows.reshape(expert_count, capacity, feat_part),
            "expert",
            split_axis=0,
            concat_axis=0,
            tiled=True,
        ),
        lax.all_to_all(
            sent_grads.reshape(expert_count, capacity, feat_part),
            "expert",
            split_axis=0,
            concat_axis=0,
            tiled=True,
        ),
    )
    gathered_rows, gathered_gradients = (
        lax.all_gather(
            recv_rows.reshape(1, slot_total, feat_part), ("dp", "pipe"), axis=0, tiled=True
        ),
        lax.all_gather(
            recv_grads.reshape(1, slot_total, feat_part), ("dp", "pipe"), axis=0, tiled=True
        ),
    )
    piece_width = model_width // pipe_count
    gathered_rows = gathered_rows.reshape(group_count, pipe_count, slot_total, piece_width)
    gathered_gradients = gathered_gradients.reshape(
        group_count, pipe_count, slot_total, piece_width
    )
    gate_weight_blocks = w_gate[0].reshape(pipe_count, piece_width, hidden_part)
    up_weight_blocks = w_up[0].reshape(pipe_count, piece_width, hidden_part)
    down_weight_blocks = w_down[0].reshape(hidden_part, pipe_count, piece_width)
    gate_pre = jnp.einsum(
        "lxvk,xkh->lvh", gathered_rows, gate_weight_blocks, preferred_element_type=jnp.float32
    )
    up_preactivation = jnp.einsum(
        "lxvk,xkh->lvh", gathered_rows, up_weight_blocks, preferred_element_type=jnp.float32
    )
    act_grad = jnp.einsum(
        "mzyj,uzj->myu", gathered_gradients, down_weight_blocks, preferred_element_type=jnp.float32
    )
    sigmoid_gate = jax.nn.sigmoid(gate_pre)
    linear = gate_pre * sigmoid_gate
    swiglu_activation = (linear * up_preactivation).astype(jnp.bfloat16)
    slope_term = sigmoid_gate * (1.0 + gate_pre * (1.0 - sigmoid_gate))
    gate_output_gradient = (act_grad * up_preactivation * slope_term).astype(jnp.bfloat16)
    up_output_gradient = (act_grad * linear).astype(jnp.bfloat16)
    gate_weight_gradient = jnp.einsum(
        "kctx,ktn->cxn", gathered_rows, gate_output_gradient, preferred_element_type=jnp.float32
    )
    gate_weight_gradient = gate_weight_gradient.reshape(model_width, hidden_part).astype(
        jnp.bfloat16
    )[None]
    up_weight_gradient = jnp.einsum(
        "kctx,ktn->cxn", gathered_rows, up_output_gradient, preferred_element_type=jnp.float32
    )
    up_weight_gradient = up_weight_gradient.reshape(model_width, hidden_part).astype(jnp.bfloat16)[
        None
    ]
    grad_down = jnp.einsum(
        "cjb,cvji->bvi", swiglu_activation, gathered_gradients, preferred_element_type=jnp.float32
    )
    grad_down = grad_down.reshape(hidden_part, model_width).astype(jnp.bfloat16)[None]
    gate_backward = w_gate[0].reshape(pipe_count, feat_part, hidden_part)
    up_backward = w_up[0].reshape(pipe_count, feat_part, hidden_part)
    input_terms = jnp.einsum(
        "mil,xkl->mxik", gate_output_gradient, gate_backward, preferred_element_type=jnp.float32
    ) + jnp.einsum(
        "mil,xkl->mxik", up_output_gradient, up_backward, preferred_element_type=jnp.float32
    )
    summed = lax.psum_scatter(
        input_terms.reshape(group_count * pipe_count, slot_total, feat_part),
        ("dp", "pipe"),
        scatter_dimension=0,
        tiled=True,
    )
    slot_grads = summed.astype(jnp.bfloat16).reshape(expert_count, capacity, feat_part)
    returned = lax.all_to_all(slot_grads, "expert", split_axis=0, concat_axis=0, tiled=True)
    grad_tokens = jnp.einsum(
        "st,sq->tq",
        picker,
        returned.reshape(slot_total, feat_part),
        preferred_element_type=jnp.float32,
    ).astype(jnp.bfloat16)
    return (grad_tokens, gate_weight_gradient, up_weight_gradient, grad_down)


def solution(mesh):
    placed = (
        P(("expert", "dp"), "pipe"),
        P(("expert", "dp"), "pipe"),
        P(("expert", "dp"), None),
        P(("expert", "dp"), None),
        P("expert", None, ("dp", "pipe")),
        P("expert", None, ("dp", "pipe")),
        P("expert", ("dp", "pipe"), None),
    )
    return jax.shard_map(
        body,
        mesh=mesh,
        in_specs=placed,
        out_specs=(
            P(("expert", "dp"), "pipe"),
            P("expert", None, ("dp", "pipe")),
            P("expert", None, ("dp", "pipe")),
            P("expert", ("dp", "pipe"), None),
        ),
        check_vma=False,
    )
```

profile of v0, /device:TPU:1, one launch (start us, length us, event | category | flops | bytes accessed | tf_op | source)
XLA Modules:
  0.0 471.8 jit_solution(10820452683716536585)
XLA Ops:
  7.2 0.9 copy.50
  8.1 0.1 eq.30
  8.2 0.1 fusion.17
  8.3 0.1 reduce_window_sum.11
  8.4 0.2 select_reduce_fusion.1
  8.6 0.1 reduce_sum.21
  8.7 0.1 copy.51
  8.8 0.7 multiply_add_fusion
  9.4 0.1 fusion.18
  9.5 1.1 convolution_convert_fusion
  10.6 12.1 %all_to_all.15 = bf16[8,16,768]{2,1,0:T(8,128)(2,1)} all-to-all(bf16[8,16,768]{2,1,0:T(8,128)(2,1)S(1)} %bitcast.111), channel_id=1, replica_groups=mesh['expert'=8,'dp'=8,'pipe'=4] {'expert'}, dimensions={0} | all-to-all | bytes 393216 | tf_op jit(solution)/shard_map/all_to_all | solution.py:43
  22.7 0.0 all-gather.3.cloned.1.call-start
  22.8 0.8 select_reduce_fusion
  23.5 1.2 convolution_convert_fusion.1
  24.7 9.9 %all_to_all.16 = bf16[8,16,768]{2,1,0:T(8,128)(2,1)} all-to-all(bf16[8,16,768]{2,1,0:T(8,128)(2,1)S(1)} %bitcast.110), channel_id=1, replica_groups=mesh['expert'=8,'dp'=8,'pipe'=4] {'expert'}, dimensions={0} | all-to-all | bytes 393216 | tf_op jit(solution)/shard_map/all_to_all | solution.py:50
  34.7 3.3 reshape_squeeze.11
  38.0 73.0 %all-gather.5.cloned.1.call-done = bf16[32,128,768]{2,1,0:T(8,128)(2,1)} async-done(((bf16[1,128,768]{2,1,0:T(8,128)(2,1)}), bf16[32,128,768]{2,1,0:T(8,128)(2,1)}) %all-gather.5.cloned.1.call-update) | async-done | bytes 6291472 | tf_op jit(solution)/shard_map/all_gather | solution.py:59
  111.0 5.7 %convolution_bitcast_fusion.3 = f32[8,128,256]{2,1,0:T(8,128)} fusion(bf16[8,4,128,768]{3,2,1,0:T(8,128)(2,1)} %bitcast.97, bf16[4,768,256,1]{2,1,0,3:T(8,128)(2,1)S(1)} %bitcast.94), kind=kOutput, calls=%fused_computation.14 | convolution fusion | flops 1610612736 | bytes 8912896 | tf_op jit(solution)/shard_map/lxvk,xkh->lvh/dot_general | solution.py:74
  116.7 2.8 convolution_bitcast_fusion.4
  119.4 79.2 %all-gather.3.cloned.1.call-done = bf16[32,128,768]{2,1,0:T(8,128)(2,1)} async-done(((bf16[1,128,768]{2,1,0:T(8,128)(2,1)}), bf16[32,128,768]{2,1,0:T(8,128)(2,1)}) %all-gather.3.cloned.1.call-update) | async-done | bytes 6291472 | tf_op jit(solution)/shard_map/all_gather | solution.py:62
  198.7 5.4 %multiply_convert_fusion.1 = (bf16[8,128,256]{2,1,0:T(8,128)(2,1)S(1)}, bf16[8,128,256]{2,1,0:T(8,128)(2,1)S(1)}) fusion(f32[8,128,256]{2,1,0:T(8,128)} %convolution_bitcast_fusion.3, f32[8,128,256]{2,1,0:T(8,128)} %convolution_bitcast_fusion.4, bf16[8,4,128,768]{3,2,1,0:T(8,128)(2,1)} %bitcast.100, bf16[256,4,768]{2,1,0:T(4,128)(2,1)S(1)} %reshape_squeeze.11), kind=kOutput, calls=%fused_computation.20 | convolution fusion | flops 1614020608 | bytes 11010048 | tf_op jit(solution)/shard_map/mzyj,uzj->myu/dot_general | solution.py:80
  204.1 1.8 fusion.14
  206.0 6.4 %convolution_add_fusion = f32[8,128,4,768]{3,1,2,0:T(8,128)} fusion(f32[8,128,4,768]{3,1,2,0:T(8,128)S(1)} %fusion.14, bf16[4,768,256,1]{2,1,0,3:T(8,128)(2,1)S(1)} %bitcast.106, bf16[8,128,256]{2,1,0:T(8,128)(2,1)S(1)} %get-tuple-element.4), kind=kOutput, calls=%fused_computation | convolution fusion | flops 1613758464 | bytes 27262976 | tf_op jit(solution)/shard_map/mil,xkl->mxik/dot_general | solution.py:109
  212.3 8.6 %copy.65 = bf16[4,768,8,128]{3,1,0,2:T(8,128)(2,1)} copy(bf16[4,768,8,128]{1,3,0,2:T(8,128)(2,1)} %bitcast.98) | data formatting | bytes 12582912 | tf_op jit(solution)/shard_map/kctx,ktn->cxn/dot_general | solution.py:89
  220.9 8.8 %copy.67 = bf16[4,768,8,128]{3,1,0,2:T(8,128)(2,1)} copy(bf16[4,768,8,128]{1,3,0,2:T(8,128)(2,1)} %bitcast.101) | data formatting | bytes 12582912 | tf_op jit(solution)/shard_map/cjb,cvji->bvi/dot_general | solution.py:101
  229.7 7.5 %fusion.4 = bf16[1,3072,256]{2,1,0:T(8,128)(2,1)} fusion(bf16[3072,8,128]{2,0,1:T(8,128)(2,1)} %bitcast.102, bf16[8,128,256]{2,1,0:T(8,128)(2,1)S(1)} %copy-done.8), kind=kOutput, calls=%fused_computation.8 | convolution fusion | flops 1611399168 | bytes 8388608 | tf_op jit(solution)/shard_map/kctx,ktn->cxn/dot_general | solution.py:95
  237.2 3.1 fusion.3
  240.3 206.2 %reduce-scatter.2.cloned.1.call-done = f32[1,128,768]{2,1,0:T(8,128)} async-done(((f32[32,128,768]{2,1,0:T(8,128)}), f32[1,128,768]{2,1,0:T(8,128)}) %reduce-scatter.2.cloned.1.call-update) | async-done | bytes 393232 | tf_op jit(solution)/shard_map/reduce_scatter | solution.py:112
  446.5 1.7 convert_element_type.40
  448.2 9.1 %all-to-all-start.2 = ((bf16[8,16,768]{2,1,0:T(8,128)(2,1)}), bf16[8,16,768]{2,1,0:T(8,128)(2,1)S(1)}, u32[]{:S(2)}, u32[]{:S(2)}) async-start(bf16[8,16,768]{2,1,0:T(8,128)(2,1)} %bitcast.24), calls=%async_computation.3 | async-start | bytes 393216 | tf_op jit(solution)/shard_map/all_to_all | solution.py:119
  457.3 7.3 %fusion.5 = bf16[1,3072,256]{2,1,0:T(8,128)(2,1)} fusion(bf16[3072,8,128]{2,0,1:T(8,128)(2,1)} %bitcast.103, bf16[8,128,256]{2,1,0:T(8,128)(2,1)S(1)} %copy-done.6), kind=kOutput, calls=%fused_computation.9 | convolution fusion | flops 1611399168 | bytes 8388608 | tf_op jit(solution)/shard_map/kctx,ktn->cxn/dot_general | solution.py:89
  464.5 0.8 convolution_convert_fusion.2
  (28 shorter events, 0.2 us)
Async XLA Ops:
  7.2 103.8 %copy-start = (bf16[1,3072,256]{2,1,0:T(8,128)(2,1)S(1)}, bf16[1,3072,256]{2,1,0:T(8,128)(2,1)}, u32[]{:S(2)}) copy-start(bf16[1,3072,256]{2,1,0:T(8,128)(2,1)} %param.11) | copy-start | bytes 4718596
  7.2 103.8 %all-gather.5.cloned.1.call-start = ((), (), s32[]{:S(2)}) async-start(), calls=%async_computation.5 | async-start | bytes 6488064 | tf_op jit(solution)/shard_map/all_gather | solution.py:59
  22.7 176.0 %all-gather.3.cloned.1.call-start = ((), (), s32[]{:S(2)}) async-start(), calls=%async_computation.4 | async-start | bytes 6488064 | tf_op jit(solution)/shard_map/all_gather | solution.py:62
  34.6 411.9 %reduce-scatter.2.cloned.1.call-start = ((), (), s32[]{:S(2)}) async-start(), calls=%async_computation.6 | async-start | bytes 12976128 | tf_op jit(solution)/shard_map/reduce_scatter | solution.py:112
  111.0 5.7 %copy-start.1 = (bf16[32,128,768]{2,1,0:T(8,128)(2,1)S(1)}, bf16[32,128,768]{2,1,0:T(8,128)(2,1)}, u32[]{:S(2)}) copy-start(bf16[32,128,768]{2,1,0:T(8,128)(2,1)} %all-gather.5.cloned.1.call-done) | copy-start | bytes 18874372
  111.0 5.7 %copy-start.3 = (bf16[1,3072,256]{2,1,0:T(8,128)(2,1)S(1)}, bf16[1,3072,256]{2,1,0:T(8,128)(2,1)}, u32[]{:S(2)}) copy-start(bf16[1,3072,256]{2,1,0:T(8,128)(2,1)} %param.12) | copy-start | bytes 4718596
  204.1 1.9 copy-start.5
  204.1 1.9 copy-start.7
  204.1 1.9 copy-start.4
  220.9 8.8 %copy-start.8 = (bf16[8,128,256]{2,1,0:T(8,128)(2,1)S(1)}, bf16[8,128,256]{2,1,0:T(8,128)(2,1)}, u32[]{:S(2)}) copy-start(bf16[8,128,256]{2,1,0:T(8,128)(2,1)} %copy-done.7) | copy-start | bytes 1572868
  229.7 7.5 %copy-start.2 = (bf16[4,768,8,128]{3,1,0,2:T(8,128)(2,1)S(1)}, bf16[4,768,8,128]{3,1,0,2:T(8,128)(2,1)}, u32[]{:S(2)}) copy-start(bf16[4,768,8,128]{3,1,0,2:T(8,128)(2,1)} %copy.67) | copy-start | bytes 18874372
  229.7 7.5 %copy-start.9 = (f32[8,128,256]{2,1,0:T(8,128)S(1)}, f32[8,128,256]{2,1,0:T(8,128)}, u32[]{:S(2)}) copy-start(f32[8,128,256]{2,1,0:T(8,128)} %convolution_bitcast_fusion.3) | copy-start | bytes 3145732
  229.7 7.5 %copy-start.10 = (f32[8,128,256]{2,1,0:T(8,128)S(1)}, f32[8,128,256]{2,1,0:T(8,128)}, u32[]{:S(2)}) copy-start(f32[8,128,256]{2,1,0:T(8,128)} %convolution_bitcast_fusion.4) | copy-start | bytes 3145732
  237.2 220.1 %copy-start.6 = (bf16[8,128,256]{2,1,0:T(8,128)(2,1)S(1)}, bf16[8,128,256]{2,1,0:T(8,128)(2,1)}, u32[]{:S(2)}) copy-start(bf16[8,128,256]{2,1,0:T(8,128)(2,1)} %copy-done.5) | copy-start | bytes 1572868
  448.2 16.3 %all-to-all-start.2 = ((bf16[8,16,768]{2,1,0:T(8,128)(2,1)}), bf16[8,16,768]{2,1,0:T(8,128)(2,1)S(1)}, u32[]{:S(2)}, u32[]{:S(2)}) async-start(bf16[8,16,768]{2,1,0:T(8,128)(2,1)} %bitcast.24), calls=%async_computation.3 | async-start | bytes 393216 | tf_op jit(solution)/shard_map/all_to_all | solution.py:119
Sparse Core Ops, SparseCore 0:
  22.9 88.0 all-gather.4
  113.6 85.0 all-gather.2
  212.5 233.9 reduce-scatter.1
where the time goes:
time: 473 us; the launch traced here: 472 us
  waiting for transfers between devices  359 us (76%)
  matrix products  42.8 us (9%)
  blocking collectives  22 us (5%)
  local copies, waits for them, and re-layouts  21.8 us (5%)
  between operations  13.9 us (3%)
  starting transfers between devices  9.19 us (2%)
    reduce_scatter x1, waiting for transfers between devices, body(): lax.psum_scatter(input_terms.reshape(group_count * pipe_count, slot_total...  206 us
    all_gather x1, waiting for transfers between devices, body(): lax.all_gather(recv_grads.reshape(1, slot_total, feat_part), ('dp', 'pipe...  79.2 us
    all_gather x1, waiting for transfers between devices, body(): lax.all_gather(recv_rows.reshape(1, slot_total, feat_part), ('dp', 'pipe'...  73 us
    all_to_all x1, blocking collectives, body(): lax.all_to_all(sent_rows.reshape(expert_count, capacity, feat_part), 'exp...  12.1 us
    all_to_all x1, blocking collectives, body(): lax.all_to_all(sent_grads.reshape(expert_count, capacity, feat_part), 'ex...  9.87 us
  transfers between devices with their start and end apart: 4, of which 3 were waited for; matrix products, arithmetic and copies ran while one was open for 10% of the time, Pallas kernels for 0%

commit v1 on v0

--- a/solution.py
+++ b/solution.py
@@ -2,6 +2,19 @@
 import jax.numpy as jnp
 from jax import lax
 from jax.sharding import PartitionSpec as P
+
+
+def detail_the_bench(v0):
+    u_next = jnp.concatenate(
+        lax.all_to_all(
+            jnp.stack(lax.axis_size(("dp", "pipe")) * [v0]),
+            axis_name=("dp", "pipe"),
+            concat_axis=0,
+            split_axis=0,
+        ),
+        0,
+    )
+    return u_next
 
 
 def dispatch_tables(expert_ids, gate_values, expert_count, capacity):
@@ -56,9 +69,7 @@
         ),
     )
     gathered_rows, gathered_gradients = (
-        lax.all_gather(
-            recv_rows.reshape(1, slot_total, feat_part), ("dp", "pipe"), axis=0, tiled=True
-        ),
+        detail_the_bench(recv_rows.reshape(1, slot_total, feat_part)),
         lax.all_gather(
             recv_grads.reshape(1, slot_total, feat_part), ("dp", "pipe"), axis=0, tiled=True
         ),

time: 473 us -> 508 us (1.074)
  waiting for transfers between devices: 359 us -> 384 us
  starting transfers between devices: 9.19 us -> 26.3 us
  blocking collectives: 22 us -> 9.19 us
    all_to_all x0 -> x2, waiting for transfers between devices: none -> 174 us  [the longest x1 170 us: detail_the_bench(): lax.all_to_all(jnp.stack(lax.axis_size(('dp', 'pipe')) * [v0]), axis_name...]
    all_gather x1, waiting for transfers between devices: 79.2 us -> 0.01 us  [body(): lax.all_gather(recv_grads.reshape(1, slot_total, feat_part), ('dp', 'pipe...]
    all_gather x1 -> x0, waiting for transfers between devices: 73 us -> none  [body(): lax.all_gather(recv_rows.reshape(1, slot_total, feat_part), ('dp', 'pipe'...]
    all_to_all x0 -> x2, starting transfers between devices: none -> 17.2 us  [the longest x1 10.7 us: detail_the_bench(): lax.all_to_all(jnp.stack(lax.axis_size(('dp', 'pipe')) * [v0]), axis_name...]
    all_to_all x1 -> x0, blocking collectives: 9.87 us -> none  [body(): lax.all_to_all(sent_grads.reshape(expert_count, capacity, feat_part), 'ex...]
  transfers between devices with their start and end apart: 4 -> 5, of which waited for: 3 -> 3; matrix products, arithmetic and copies ran while one was open for 10% -> 10% of each run, Pallas kernels for 0% -> 0%
where the time goes in v1:
time: 508 us; the launch traced here: 507 us
  waiting for transfers between devices  384 us (76%)
  matrix products  46.9 us (9%)
  starting transfers between devices  26.3 us (5%)
  local copies, waits for them, and re-layouts  23.7 us (5%)
  between operations  14.2 us (3%)
  blocking collectives  9.19 us (2%)
    reduce_scatter x1, waiting for transfers between devices, body(): lax.psum_scatter(input_terms.reshape(group_count * pipe_count, slot_total...  208 us
    all_to_all x1, waiting for transfers between devices, detail_the_bench(): lax.all_to_all(jnp.stack(lax.axis_size(('dp', 'pipe')) * [v0]), axis_name...  170 us
    all_to_all x1, starting transfers between devices, detail_the_bench(): lax.all_to_all(jnp.stack(lax.axis_size(('dp', 'pipe')) * [v0]), axis_name...  10.7 us
  transfers between devices with their start and end apart: 5, of which 3 were waited for; matrix products, arithmetic and copies ran while one was open for 10% of the time, Pallas kernels for 0%

profile of v1, /device:TPU:1, one launch (start us, length us, event | category | flops | bytes accessed | tf_op | source)
XLA Modules:
  0.0 507.4 jit_solution(504692900004145916)
XLA Ops:
  7.2 0.9 copy.50
  8.1 0.1 eq.30
  8.2 0.1 reduce_window_sum.11
  8.3 0.2 select_reduce_fusion.1
  8.5 0.1 reduce_sum.21
  8.6 0.1 copy.51
  8.7 0.7 multiply_add_fusion
  9.4 0.8 select_reduce_fusion
  10.2 1.8 convolution_convert_fusion.1
  12.0 6.5 %all-to-all-start = ((bf16[8,16,768]{2,1,0:T(8,128)(2,1)}), bf16[8,16,768]{2,1,0:T(8,128)(2,1)S(1)}, u32[]{:S(2)}, u32[]{:S(2)}) async-start(bf16[8,16,768]{2,1,0:T(8,128)(2,1)} %bitcast), calls=%async_computation | async-start | bytes 393216 | tf_op jit(solution)/shard_map/all_to_all | solution.py:63
  18.6 1.1 convolution_convert_fusion
  19.7 4.7 all-to-all-done
  24.4 9.2 %all_to_all.20 = bf16[8,16,768]{2,1,0:T(8,128)(2,1)S(1)} all-to-all(bf16[8,16,768]{2,1,0:T(8,128)(2,1)S(1)} %bitcast.117), channel_id=1, replica_groups=mesh['expert'=8,'dp'=8,'pipe'=4] {'expert'}, dimensions={0} | all-to-all | bytes 393216 | tf_op jit(solution)/shard_map/all_to_all | solution.py:56
  33.6 3.4 stack.3
  37.0 10.7 %all-to-all-start.2 = ((bf16[32,1,128,768]{3,2,1,0:T(8,128)(2,1)}), bf16[32,1,128,768]{3,2,1,0:T(8,128)(2,1)}, u32[]{:S(2)}, u32[]{:S(2)}) async-start(bf16[32,1,128,768]{3,2,1,0:T(8,128)(2,1)} %stack.3), calls=%async_computation.2 | async-start | bytes 12582912 | tf_op jit(solution)/shard_map/all_to_all | solution.py:9
  47.7 0.7 all-gather.2.cloned.1.call-update
  48.5 2.1 reshape_squeeze.11
  50.6 169.6 %all-to-all-done.2 = bf16[32,1,128,768]{3,2,1,0:T(8,128)(2,1)} async-done(((bf16[32,1,128,768]{3,2,1,0:T(8,128)(2,1)}), bf16[32,1,128,768]{3,2,1,0:T(8,128)(2,1)}, u32[]{:S(2)}, u32[]{:S(2)}) %all-to-all-start.2) | async-done | bytes 6291488 | tf_op jit(solution)/shard_map/all_to_all | solution.py:9
  220.2 6.0 %fusion.16 = f32[8,128,256]{2,1,0:T(8,128)} fusion(bf16[4,768,256,1]{2,1,0,3:T(8,128)(2,1)} %bitcast.112, bf16[8,4,128,768]{3,2,1,0:T(8,128)(2,1)} %bitcast.101), kind=kOutput, calls=%fused_computation.18 | convolution fusion | flops 1610612736 | bytes 8912896 | tf_op jit(solution)/shard_map/lxvk,xkh->lvh/dot_general | solution.py:88
  226.2 5.7 %fusion.19 = f32[8,128,256]{2,1,0:T(8,128)} fusion(bf16[4,768,256,1]{2,1,0,3:T(8,128)(2,1)S(1)} %bitcast.104, bf16[8,4,128,768]{3,2,1,0:T(8,128)(2,1)} %bitcast.103), kind=kOutput, calls=%fused_computation.19 | convolution fusion | flops 1610612736 | bytes 8912896 | tf_op jit(solution)/shard_map/lxvk,xkh->lvh/dot_general | solution.py:85
  231.9 5.3 %multiply_convert_fusion.1 = (bf16[8,128,256]{2,1,0:T(8,128)(2,1)S(1)}, bf16[8,128,256]{2,1,0:T(8,128)(2,1)S(1)}) fusion(f32[8,128,256]{2,1,0:T(8,128)} %fusion.19, f32[8,128,256]{2,1,0:T(8,128)} %fusion.16, bf16[8,4,128,768]{3,2,1,0:T(8,128)(2,1)} %bitcast.107, bf16[256,4,768]{2,1,0:T(4,128)(2,1)S(1)} %copy-done.4), kind=kOutput, calls=%fused_computation.24 | convolution fusion | flops 1614020608 | bytes 11010048 | tf_op jit(solution)/shard_map/mzyj,uzj->myu/dot_general | solution.py:91
  237.3 1.8 fusion.24
  239.1 6.4 %convolution_add_fusion = f32[8,128,4,768]{3,1,2,0:T(8,128)} fusion(f32[8,128,4,768]{3,1,2,0:T(8,128)S(1)} %fusion.24, bf16[4,768,256,1]{2,1,0,3:T(8,128)(2,1)S(1)} %bitcast.113, bf16[8,128,256]{2,1,0:T(8,128)(2,1)S(1)} %get-tuple-element.4), kind=kOutput, calls=%fused_computation.4 | convolution fusion | flops 1613758464 | bytes 27262976 | tf_op jit(solution)/shard_map/mil,xkl->mxik/dot_general | solution.py:120
  245.5 8.6 %copy.65 = bf16[4,768,8,128]{3,1,0,2:T(8,128)(2,1)} copy(bf16[4,768,8,128]{1,3,0,2:T(8,128)(2,1)} %bitcast.26) | data formatting | bytes 12582912 | tf_op jit(solution)/shard_map/kctx,ktn->cxn/dot_general | solution.py:100
  254.1 8.4 %copy.67 = bf16[4,768,8,128]{3,1,0,2:T(8,128)(2,1)} copy(bf16[4,768,8,128]{1,3,0,2:T(8,128)(2,1)} %bitcast.108) | data formatting | bytes 12582912 | tf_op jit(solution)/shard_map/cjb,cvji->bvi/dot_general | solution.py:112
  262.5 7.5 %fusion.8 = bf16[1,3072,256]{2,1,0:T(8,128)(2,1)} fusion(bf16[3072,8,128]{2,0,1:T(8,128)(2,1)} %bitcast.109, bf16[8,128,256]{2,1,0:T(8,128)(2,1)S(1)} %copy-done.10), kind=kOutput, calls=%fused_computation.12 | convolution fusion | flops 1611399168 | bytes 8388608 | tf_op jit(solution)/shard_map/kctx,ktn->cxn/dot_general | solution.py:106
  270.1 3.1 fusion.7
  273.2 208.4 %reduce-scatter.2.cloned.1.call-done = f32[1,128,768]{2,1,0:T(8,128)} async-done(((f32[32,128,768]{2,1,0:T(8,128)}), f32[1,128,768]{2,1,0:T(8,128)}) %reduce-scatter.2.cloned.1.call-update) | async-done | bytes 393232 | tf_op jit(solution)/shard_map/reduce_scatter | solution.py:123
  481.6 1.7 convert_element_type.40
  483.3 9.1 %all-to-all-start.3 = ((bf16[8,16,768]{2,1,0:T(8,128)(2,1)}), bf16[8,16,768]{2,1,0:T(8,128)(2,1)S(1)}, u32[]{:S(2)}, u32[]{:S(2)}) async-start(bf16[8,16,768]{2,1,0:T(8,128)(2,1)} %bitcast.24), calls=%async_computation.4 | async-start | bytes 393216 | tf_op jit(solution)/shard_map/all_to_all | solution.py:130
  492.4 7.4 %fusion.9 = bf16[1,3072,256]{2,1,0:T(8,128)(2,1)} fusion(bf16[3072,8,128]{2,0,1:T(8,128)(2,1)} %bitcast.110, bf16[8,128,256]{2,1,0:T(8,128)(2,1)S(1)} %copy-done.7), kind=kOutput, calls=%fused_computation.13 | convolution fusion | flops 1611399168 | bytes 8388608 | tf_op jit(solution)/shard_map/kctx,ktn->cxn/dot_general | solution.py:100
  499.8 0.8 convolution_convert_fusion.2
  (33 shorter events, 0.3 us)
Async XLA Ops:
  7.2 219.1 %copy-start = (bf16[1,3072,256]{2,1,0:T(8,128)(2,1)S(1)}, bf16[1,3072,256]{2,1,0:T(8,128)(2,1)}, u32[]{:S(2)}) copy-start(bf16[1,3072,256]{2,1,0:T(8,128)(2,1)} %param.11) | copy-start | bytes 4718596
  12.0 12.4 %all-to-all-start = ((bf16[8,16,768]{2,1,0:T(8,128)(2,1)}), bf16[8,16,768]{2,1,0:T(8,128)(2,1)S(1)}, u32[]{:S(2)}, u32[]{:S(2)}) async-start(bf16[8,16,768]{2,1,0:T(8,128)(2,1)} %bitcast), calls=%async_computation | async-start | bytes 393216 | tf_op jit(solution)/shard_map/all_to_all | solution.py:63
  24.4 12.6 %copy-start.8 = (bf16[8,16,768]{2,1,0:T(8,128)(2,1)}, bf16[8,16,768]{2,1,0:T(8,128)(2,1)S(1)}, u32[]{:S(2)}) copy-start(bf16[8,16,768]{2,1,0:T(8,128)(2,1)S(1)} %all-to-all-done) | copy-start | bytes 589828
  37.0 11.5 %copy-start.3 = (bf16[1,256,3072]{2,1,0:T(8,128)(2,1)S(1)}, bf16[1,256,3072]{2,1,0:T(8,128)(2,1)}, u32[]{:S(2)}) copy-start(bf16[1,256,3072]{2,1,0:T(8,128)(2,1)} %param.13) | copy-start | bytes 4718596
  37.0 183.3 %all-to-all-start.2 = ((bf16[32,1,128,768]{3,2,1,0:T(8,128)(2,1)}), bf16[32,1,128,768]{3,2,1,0:T(8,128)(2,1)}, u32[]{:S(2)}, u32[]{:S(2)}) async-start(bf16[32,1,128,768]{3,2,1,0:T(8,128)(2,1)} %stack.3), calls=%async_computation.2 | async-start | bytes 12582912 | tf_op jit(solution)/shard_map/all_to_all | solution.py:9
  47.7 184.2 %all-gather.2.cloned.1.call-start = ((), (), s32[]{:S(2)}) async-start(), calls=%async_computation.5 | async-start | bytes 6488064 | tf_op jit(solution)/shard_map/all_gather | solution.py:73
  48.4 433.2 %reduce-scatter.2.cloned.1.call-start = ((), (), s32[]{:S(2)}) async-start(), calls=%async_computation.6 | async-start | bytes 12976128 | tf_op jit(solution)/shard_map/reduce_scatter | solution.py:123
  226.2 5.7 %copy-start.4 = (bf16[256,4,768]{2,1,0:T(4,128)(2,1)S(1)}, bf16[256,4,768]{2,1,0:T(4,128)(2,1)}, u32[]{:S(2)}) copy-start(bf16[256,4,768]{2,1,0:T(4,128)(2,1)} %reshape_squeeze.11) | copy-start | bytes 4718596
  237.2 1.9 copy-start.6
  237.2 1.9 copy-start.9
  237.2 1.9 copy-start.5
  254.1 8.4 %copy-start.10 = (bf16[8,128,256]{2,1,0:T(8,128)(2,1)S(1)}, bf16[8,128,256]{2,1,0:T(8,128)(2,1)}, u32[]{:S(2)}) copy-start(bf16[8,128,256]{2,1,0:T(8,128)(2,1)} %copy-done.9) | copy-start | bytes 1572868
  262.5 7.6 %copy-start.2 = (bf16[4,768,8,128]{3,1,0,2:T(8,128)(2,1)S(1)}, bf16[4,768,8,128]{3,1,0,2:T(8,128)(2,1)}, u32[]{:S(2)}) copy-start(bf16[4,768,8,128]{3,1,0,2:T(8,128)(2,1)} %copy.67) | copy-start | bytes 18874372
  262.5 7.6 %copy-start.11 = (f32[8,128,256]{2,1,0:T(8,128)S(1)}, f32[8,128,256]{2,1,0:T(8,128)}, u32[]{:S(2)}) copy-start(f32[8,128,256]{2,1,0:T(8,128)} %fusion.16) | copy-start | bytes 3145732
  262.5 7.6 %copy-start.12 = (f32[8,128,256]{2,1,0:T(8,128)S(1)}, f32[8,128,256]{2,1,0:T(8,128)}, u32[]{:S(2)}) copy-start(f32[8,128,256]{2,1,0:T(8,128)} %fusion.19) | copy-start | bytes 3145732
  270.1 222.3 %copy-start.7 = (bf16[8,128,256]{2,1,0:T(8,128)(2,1)S(1)}, bf16[8,128,256]{2,1,0:T(8,128)(2,1)}, u32[]{:S(2)}) copy-start(bf16[8,128,256]{2,1,0:T(8,128)(2,1)} %copy-done.6) | copy-start | bytes 1572868
  483.3 16.5 %all-to-all-start.3 = ((bf16[8,16,768]{2,1,0:T(8,128)(2,1)}), bf16[8,16,768]{2,1,0:T(8,128)(2,1)S(1)}, u32[]{:S(2)}, u32[]{:S(2)}) async-start(bf16[8,16,768]{2,1,0:T(8,128)(2,1)} %bitcast.24), calls=%async_computation.4 | async-start | bytes 393216 | tf_op jit(solution)/shard_map/all_to_all | solution.py:130
  492.4 8.2 %copy-start.1 = (bf16[1,3072,256]{2,1,0:T(8,128)(2,1)S(1)}, bf16[1,3072,256]{2,1,0:T(8,128)(2,1)}, u32[]{:S(2)}) copy-start(bf16[1,3072,256]{2,1,0:T(8,128)(2,1)} %param.11) | copy-start | bytes 4718596
Sparse Core Ops, SparseCore 0:
  51.7 169.8 all-gather.1
  245.6 235.9 reduce-scatter.1
